TPU v7x, 32 devices: a whole 2x2x4 slice. The times are simulated.
32 devices in a mesh: sensor: 8 (over y, x, core), tm: 4 (over z).
Axes of the slice: x: 2, y: 2, z: 4, core: 2. Of those that a mesh axis runs over, the one named last changes fastest.
Arguments:
- series: bfloat16 [12, 1024, 128], P('tm', 'sensor'), may hold values from -40 to 40
- conv_weight: bfloat16 [3, 128, 256], replicated, may hold values from -0.3125 to 0.3125
- qk_weight: bfloat16 [2, 128, 128], replicated, may hold values from -1 to 1
- value_weight: bfloat16 [128, 128], replicated, may hold values from -0.5 to 0.5
- out_weight: bfloat16 [128, 128], replicated, may hold values from -0.5 to 0.5
- norm_gain: float32 [128], replicated, may hold values from 0.25 to 1.75
Outputs:
- layer_out: bfloat16 [12, 1024, 128], P('tm', 'sensor')
All inputs are finite; a program needn't handle non-finite values.
Results may differ from a plain program's by a relative error of at most 0.012.
The roundings to bfloat16 on the way count: a program that leaves them out, or rounds other values in their place, can miss the bound.
Values may be sent and summed in bfloat16 or wider, within the bound.
A program may use at most 64 MiB of HBM per device.

v0:
```python
import math

import jax
import jax.numpy as jnp
from jax import lax
from jax.sharding import PartitionSpec as P

HEADS = 8


def from_behind(block, axis, distance):
    devices = range(lax.axis_size(axis))
    route = [(i - distance, i) for i in devices if i - distance in devices]
    return lax.ppermute(block, axis, route)


def local(series, conv_weight, qk_weight, value_weight, out_weight, norm_gain):
    steps_dev, sens_dev, width = series.shape
    head_dim = width // HEADS
    scale = 1.0 / math.sqrt(head_dim)
    taps = conv_weight.shape[0]
    rows = steps_dev * sens_dev
    earlier = from_behind(series[steps_dev - (taps - 1) :], "tm", 1)
    padded = jnp.concatenate([earlier, series], axis=0)
    conv = jnp.zeros((rows, 2 * width), jnp.float32)
    for tap in range(taps):
        window = padded[taps - 1 - tap : taps - 1 - tap + steps_dev].reshape(rows, width)
        conv = conv + jnp.dot(window, conv_weight[tap], preferred_element_type=jnp.float32)
    flat = series.reshape(rows, width).astype(jnp.float32)
    hidden = (flat + conv[:, :width] * jax.nn.sigmoid(conv[:, width:])).astype(jnp.bfloat16)
    query = jnp.dot(hidden, qk_weight[0], preferred_element_type=jnp.float32).astype(jnp.bfloat16)
    query = query.reshape(steps_dev, sens_dev, HEADS, head_dim)

    def absorb_block(carry, keys, values):
        maxima, totals, summed = carry
        count = keys.shape[1]
        keys = keys.reshape(steps_dev, count, HEADS, head_dim)
        values = values.reshape(steps_dev, count, HEADS, head_dim)
        scores = (
            jnp.einsum("tshd,tkhd->thsk", query, keys, preferred_element_type=jnp.float32) * scale
        )
        new_max = jnp.maximum(maxima, jnp.max(scores, axis=-1))
        correct = jnp.exp(maxima - new_max)
        probs = jnp.exp(scores - new_max[..., None])
        totals = totals * correct + jnp.sum(probs, axis=-1)
        added = jnp.einsum(
            "thsk,tkhd->thsd",
            probs.astype(jnp.bfloat16),
            values,
            preferred_element_type=jnp.float32,
        )
        summed = summed * correct[..., None] + added
        return (new_max, totals, summed)

    start_state = (
        jnp.full((steps_dev, HEADS, sens_dev), -1e30, jnp.float32),
        jnp.zeros((steps_dev, HEADS, sens_dev), jnp.float32),
        jnp.zeros((steps_dev, HEADS, sens_dev, head_dim), jnp.float32),
    )
    source = hidden.reshape(steps_dev, sens_dev, width)
    count = source.shape[1]
    source_rows = source.reshape(steps_dev * count, width)
    keys = jnp.dot(source_rows, qk_weight[1], preferred_element_type=jnp.float32).astype(
        jnp.bfloat16
    )
    values = jnp.dot(source_rows, value_weight, preferred_element_type=jnp.float32).astype(
        jnp.bfloat16
    )
    own_keys = keys.reshape(steps_dev, count, width)
    own_values = values.reshape(steps_dev, count, width)
    keys = lax.all_gather(own_keys, "sensor", axis=1, tiled=True)
    count = keys.shape[1]
    block = math.gcd(count, 512)
    nblocks = count // block
    key_blocks = jnp.moveaxis(keys.reshape(steps_dev, nblocks, block, width), 1, 0)
    value_blocks = jnp.moveaxis(
        lax.all_gather(own_values, "sensor", axis=1, tiled=True).reshape(
            steps_dev, nblocks, block, width
        ),
        1,
        0,
    )

    def one_turn(state, pair):
        return (absorb_block(state, pair[0], pair[1]), None)

    final, unused = lax.scan(one_turn, start_state, (key_blocks, value_blocks))
    maxima, totals, summed = final
    attended = summed / totals[..., None]
    attended = jnp.transpose(attended, (0, 2, 1, 3)).reshape(rows, width).astype(jnp.bfloat16)
    mixed = jnp.dot(attended, out_weight, preferred_element_type=jnp.float32) + hidden.astype(
        jnp.float32
    )
    mean = jnp.mean(mixed, axis=-1, keepdims=True)
    var = jnp.mean((mixed - mean) ** 2, axis=-1, keepdims=True)
    normed = (mixed - mean) / jnp.sqrt(var + 1e-05) * norm_gain
    return normed.reshape(steps_dev, sens_dev, width).astype(jnp.bfloat16)


def solution(mesh):
    in_specs = (P("tm", "sensor", None), P(), P(), P(), P(), P())
    out_specs = P("tm", "sensor", None)
    return jax.shard_map(local, mesh=mesh, in_specs=in_specs, out_specs=out_specs, check_vma=False)
```

profile of v0, /device:TPU:0, one launch (start us, length us, event | category | flops | bytes accessed | tf_op | source)
XLA Modules:
  0.0 44.4 jit_solution(14580091895317619803)
XLA Ops:
  0.0 0.0 copy-start
  0.0 0.9 %slice.31 = bf16[2,128,128]{2,1,0:T(8,128)(2,1)S(1)} slice(bf16[3,128,128]{2,1,0:T(8,128)(2,1)} %param.8), slice={[1:3], [0:128], [0:128]} | slice | bytes 131072 | tf_op jit(solution)/shard_map/slice | solution.py:23
  0.9 4.9 %collective-permute-start = (bf16[2,128,128]{2,1,0:T(8,128)(2,1)S(1)}, bf16[2,128,128]{2,1,0:T(8,128)(2,1)S(1)}, u32[]{:S(2)}, u32[]{:S(2)}) collective-permute-start(bf16[2,128,128]{2,1,0:T(8,128)(2,1)S(1)} %slice.31), channel_id=1, source_target_pairs={{0,1},{1,2},{2,3},{4,5},{5,6},{6,7},{8,9},{9,10},{10,11},{12,13},{... | collective-permute-start | bytes 196616 | tf_op jit(solution)/shard_map/ppermute | solution.py:14
  5.8 1.1 %fusion.21 = f32[384,256]{1,0:T(8,128)S(1)} fusion(bf16[384,128]{1,0:T(8,128)(2,1)} %bitcast.86, bf16[3,128,256]{2,1,0:T(8,128)(2,1)} %param.9), kind=kOutput, calls=%fused_computation.36 | convolution fusion | flops 25165824 | bytes 557056 | tf_op jit(solution)/shard_map/dot_general | solution.py:28
  6.9 0.8 %collective-permute-done = bf16[2,128,128]{2,1,0:T(8,128)(2,1)S(1)} collective-permute-done((bf16[2,128,128]{2,1,0:T(8,128)(2,1)S(1)}, bf16[2,128,128]{2,1,0:T(8,128)(2,1)S(1)}, u32[]{:S(2)}, u32[]{:S(2)}) %collective-permute-start) | collective-permute-done | bytes 65568 | tf_op jit(solution)/shard_map/ppermute | solution.py:14
  7.7 0.9 %constant_dynamic-update-slice_fusion = bf16[5,128,128]{2,1,0:T(8,128)(2,1)S(1)} fusion(bf16[5,128,128]{2,1,0:T(8,128)(2,1)S(1)} %constant_dynamic-update-slice_fusion.1, bf16[3,128,128]{2,1,0:T(8,128)(2,1)} %param.8), kind=kLoop, calls=%fused_computation.45 | loop fusion | bytes 196608 | tf_op jit(solution)/shard_map/concatenate | solution.py:24
  8.6 1.0 %convolution_add_fusion.1 = f32[384,256]{1,0:T(8,128)S(1)} fusion(f32[384,256]{1,0:T(8,128)S(1)} %fusion.21, bf16[384,128]{1,0:T(8,128)(2,1)S(1)} %bitcast.91, bf16[3,128,256]{2,1,0:T(8,128)(2,1)} %param.9), kind=kOutput, calls=%fused_computation.16 | convolution fusion | flops 25264128 | bytes 950272 | tf_op jit(solution)/shard_map/dot_general | solution.py:28
  9.7 1.0 %convolution_add_fusion = f32[384,256]{1,0:T(8,128)S(1)} fusion(f32[384,256]{1,0:T(8,128)S(1)} %convolution_add_fusion.1, bf16[384,128]{1,0:T(8,128)(2,1)S(1)} %bitcast.90, bf16[3,128,256]{2,1,0:T(8,128)(2,1)} %param.9), kind=kOutput, calls=%fused_computation.15 | convolution fusion | flops 25264128 | bytes 950272 | tf_op jit(solution)/shard_map/dot_general | solution.py:28
  10.7 1.0 %fusion.15 = bf16[384,128]{1,0:T(8,128)(2,1)S(1)} fusion(f32[384,256]{1,0:T(8,128)S(1)} %convolution_add_fusion, bf16[3,128,128]{2,1,0:T(8,128)(2,1)} %param.8), kind=kLoop, calls=%fused_computation.30 | loop fusion | flops 344064 | bytes 589824 | tf_op jit(solution)/shard_map/convert_element_type | solution.py:30
  11.7 0.9 %convolution_convert_fusion.1 = bf16[384,128]{1,0:T(8,128)(2,1)S(1)} fusion(bf16[384,128]{1,0:T(8,128)(2,1)S(1)} %fusion.15, bf16[2,128,128]{2,1,0:T(8,128)(2,1)} %param.10), kind=kOutput, calls=%fused_computation.19 | convolution fusion | flops 12632064 | bytes 229376 | tf_op jit(solution)/shard_map/dot_general | solution.py:31
  12.6 0.9 %convolution_convert_fusion.2 = bf16[384,128]{1,0:T(8,128)(2,1)S(1)} fusion(bf16[384,128]{1,0:T(8,128)(2,1)S(1)} %fusion.15, bf16[2,128,128]{2,1,0:T(8,128)(2,1)} %param.10), kind=kOutput, calls=%fused_computation.20 | convolution fusion | flops 12632064 | bytes 229376 | tf_op jit(solution)/shard_map/dot_general | solution.py:63
  13.5 0.9 %convolution_convert_fusion = bf16[384,128]{1,0:T(8,128)(2,1)S(1)} fusion(bf16[384,128]{1,0:T(8,128)(2,1)S(1)} %fusion.15, bf16[128,128]{1,0:T(8,128)(2,1)} %param.11), kind=kOutput, calls=%fused_computation.18 | convolution fusion | flops 12632064 | bytes 229376 | tf_op jit(solution)/shard_map/dot_general | solution.py:66
  14.4 0.1 copy.10
  14.6 10.4 %all_gather.6 = bf16[3,1024,128]{2,1,0:T(8,128)(2,1)S(1)} all-gather(bf16[3,128,128]{2,1,0:T(8,128)(2,1)S(1)} %bitcast.89), channel_id=1, replica_groups=mesh['sensor'=8,'tm'=4] {'sensor'}, dimensions={1}, use_global_device_ids=true | all-gather | bytes 884736 | tf_op jit(solution)/shard_map/all_gather | solution.py:71
  25.1 10.4 %all_gather.7 = bf16[3,1024,128]{2,1,0:T(8,128)(2,1)S(1)} all-gather(bf16[3,128,128]{2,1,0:T(8,128)(2,1)S(1)} %bitcast.88), channel_id=1, replica_groups=mesh['sensor'=8,'tm'=4] {'sensor'}, dimensions={1}, use_global_device_ids=true | all-gather | bytes 884736 | tf_op jit(solution)/shard_map/all_gather | solution.py:77
  35.4 0.0 copy-start.1
  35.4 7.4 %while.15 = (s32[]{:T(128)}, f32[3,8,128]{2,1,0:T(8,128)S(1)}, f32[3,8,128]{2,1,0:T(8,128)S(1)}, f32[3,8,128,16]{2,3,1,0:T(8,128)S(1)}, bf16[2,3,512,128]{3,2,0,...) while((s32[]{:T(128)}, f32[3,8,128]{2,1,0:T(8,128)S(1)}, ...), condition=%wide.region_3.4_spmd.clone, body=%wide.region_0.3_spmd.clone.sunk | while | flops 113409024 | bytes 23494772 | solution.py:87
  35.4 0.1 constant_dynamic-slice_fusion.3
  35.5 0.2 copy.27
  35.7 0.2 copy.28
  35.9 1.1 %bitcast_reduce_fusion.2 = (f32[3,8,128]{2,1,0:T(8,128)S(1)}, f32[3,8,512,128]{3,2,1,0:T(8,128)S(1)}) fusion(bf16[3,512,8,16]{1,3,2,0:T(8,128)(2,1)S(1)} %bitcast.83, bf16[3,128,8,16]{1,3,2,0:T(8,128)(2,1)S(1)} %get-tuple-element.185), kind=kOutput, calls=%fused_computation.1.clone.1 | convolution fusion | flops 53474304 | bytes 6795264 | tf_op jit(solution)/shard_map/while/body/eval_jaxpr/tshd,tkhd->thsk/dot_general | solution.py:40
  37.0 1.1 %fusion.54 = f32[3,8,128]{2,1,0:T(8,128)S(1)} fusion(f32[3,8,512,128]{3,2,1,0:T(8,128)S(1)} %get-tuple-element.158, f32[3,8,128]{2,1,0:T(8,128)S(1)} %select_maximum_fusion.2), kind=kLoop, calls=%fused_computation.4.clone.1 | loop fusion | flops 4715520 | bytes 6316032 | tf_op jit(solution)/shard_map/while/body/eval_jaxpr/reduce_sum | solution.py:45
  38.0 1.1 %fusion.56 = f32[3,8,128,16]{2,3,1,0:T(8,128)S(1)} fusion(bf16[3,512,8,16]{1,3,2,0:T(8,128)(2,1)S(1)} %bitcast.82, f32[3,8,512,128]{3,2,1,0:T(8,128)S(1)} %get-tuple-element.158, f32[3,8,128]{2,1,0:T(8,128)S(1)} %select_maximum_fusion.2, f32[3,8,128,16]{2,3,1,0:T(8,128)S(1)} %get-tuple-element.174, f32[3,8,128]{2,1,0:T(8,128)S(1)} %get-tuple-element.161, ...), kind=kOutput, calls=%fused_computation.6.clone.1 | convolution fusion | flops 55197696 | bytes 7102465 | tf_op jit(solution)/shard_map/while/body/eval_jaxpr/thsk,tkhd->thsd/dot_general | solution.py:46
  39.1 0.1 constant_dynamic-slice_fusion.3
  39.2 0.2 copy.27
  39.4 0.2 copy.28
  39.6 1.1 %bitcast_reduce_fusion.2 = (f32[3,8,128]{2,1,0:T(8,128)S(1)}, f32[3,8,512,128]{3,2,1,0:T(8,128)S(1)}) fusion(bf16[3,512,8,16]{1,3,2,0:T(8,128)(2,1)S(1)} %bitcast.83, bf16[3,128,8,16]{1,3,2,0:T(8,128)(2,1)S(1)} %get-tuple-element.185), kind=kOutput, calls=%fused_computation.1.clone.1 | convolution fusion | flops 53474304 | bytes 6795264 | tf_op jit(solution)/shard_map/while/body/eval_jaxpr/tshd,tkhd->thsk/dot_general | solution.py:40
  40.6 1.1 %fusion.54 = f32[3,8,128]{2,1,0:T(8,128)S(1)} fusion(f32[3,8,512,128]{3,2,1,0:T(8,128)S(1)} %get-tuple-element.158, f32[3,8,128]{2,1,0:T(8,128)S(1)} %select_maximum_fusion.2), kind=kLoop, calls=%fused_computation.4.clone.1 | loop fusion | flops 4715520 | bytes 6316032 | tf_op jit(solution)/shard_map/while/body/eval_jaxpr/reduce_sum | solution.py:45
  41.7 1.1 %fusion.56 = f32[3,8,128,16]{2,3,1,0:T(8,128)S(1)} fusion(bf16[3,512,8,16]{1,3,2,0:T(8,128)(2,1)S(1)} %bitcast.82, f32[3,8,512,128]{3,2,1,0:T(8,128)S(1)} %get-tuple-element.158, f32[3,8,128]{2,1,0:T(8,128)S(1)} %select_maximum_fusion.2, f32[3,8,128,16]{2,3,1,0:T(8,128)S(1)} %get-tuple-element.174, f32[3,8,128]{2,1,0:T(8,128)S(1)} %get-tuple-element.161, ...), kind=kOutput, calls=%fused_computation.6.clone.1 | convolution fusion | flops 55197696 | bytes 7102465 | tf_op jit(solution)/shard_map/while/body/eval_jaxpr/thsk,tkhd->thsd/dot_general | solution.py:46
  42.8 0.1 copy.14
  42.9 0.0 copy-done
  43.0 0.3 fusion.31
  43.3 0.2 multiply_reduce_fusion
  43.5 0.0 copy-done.1
  43.5 0.8 %multiply_convert_fusion = bf16[384,128]{1,0:T(8,128)(2,1)} fusion(f32[384,128]{1,0:T(8,128)S(1)} %get-tuple-element.106, f32[128]{0:T(128)S(1)} %copy-done.1, f32[384]{0:T(512)S(1)} %add_sqrt_fusion, f32[384]{0:T(512)S(1)} %broadcast_multiply_fusion), kind=kLoop, calls=%fused_computation.27 | loop fusion | flops 196608 | bytes 298496 | tf_op jit(solution)/shard_map/convert_element_type | solution.py:97
  (16 shorter events, 0.2 us)
Async XLA Ops:
  0.0 42.9 %copy-start = (bf16[128,128]{1,0:T(8,128)(2,1)S(1)}, bf16[128,128]{1,0:T(8,128)(2,1)}, u32[]{:S(2)}) copy-start(bf16[128,128]{1,0:T(8,128)(2,1)} %param.12) | copy-start | bytes 98308
  0.9 6.8 %collective-permute-start = (bf16[2,128,128]{2,1,0:T(8,128)(2,1)S(1)}, bf16[2,128,128]{2,1,0:T(8,128)(2,1)S(1)}, u32[]{:S(2)}, u32[]{:S(2)}) collective-permute-start(bf16[2,128,128]{2,1,0:T(8,128)(2,1)S(1)} %slice.31), channel_id=1, source_target_pairs={{0,1},{1,2},{2,3},{4,5},{5,6},{6,7},{8,9},{9,10},{10,11},{12,13},{... | collective-permute-start | bytes 196616 | tf_op jit(solution)/shard_map/ppermute | solution.py:14
  35.4 8.1 %copy-start.1 = (f32[128]{0:T(128)S(1)}, f32[128]{0:T(128)}, u32[]{:S(2)}) copy-start(f32[128]{0:T(128)} %param.13) | copy-start | bytes 1540
where the time goes:
time: 45 us; the launch traced here: 44.4 us
  blocking collectives  20.8 us (46%)
  matrix products  10.5 us (23%)
  starting transfers between devices  4.95 us (11%)
  other arithmetic  4.22 us (9%)
  local copies, waits for them, and re-layouts  2.89 us (6%)
  waiting for transfers between devices  0.77 us (2%)
    all_gather x1, blocking collectives, local(): keys = lax.all_gather(own_keys, 'sensor', axis=1, tiled=True)  10.4 us
    all_gather x1, blocking collectives, local(): lax.all_gather(own_values, 'sensor', axis=1, tiled=True)  10.4 us
    ppermute x1, starting transfers between devices, from_behind(): return lax.ppermute(block, axis, route)  4.95 us
    dot_general x3, matrix products, local(): jnp.dot(window, conv_weight[tap], preferred_element_type=jnp.float32)  3.13 us
    dot_general x2, matrix products, absorb_block(): jnp.einsum('tshd,tkhd->thsk', query, keys, preferred_element_type=jnp.flo...  2.16 us
    dot_general x2, matrix products, absorb_block(): jnp.einsum('thsk,tkhd->thsd', probs.astype(jnp.bfloat16), values, preferr...  2.15 us
    reduce_sum x2, other arithmetic, absorb_block(): totals = totals * correct + jnp.sum(probs, axis=-1)  2.12 us
    convert_element_type x1, other arithmetic, local(): (flat + conv[:, :width] * jax.nn.sigmoid(conv[:, width:])).astype(jnp.bfl...  0.96 us
  transfers between devices with their start and end apart: 1, of which 1 were waited for; matrix products, arithmetic and copies ran while one was open for 2% of the time, Pallas kernels for 0%

commit v1 on v0

v1 whole, which is shorter than its diff:
```python
import functools
import math

import jax
import jax.numpy as jnp
from jax import lax
from jax.experimental import pallas as pl
from jax.experimental.pallas import tpu as pltpu
from jax.sharding import PartitionSpec as P

HEADS = 8
MESH = pl.DeviceIdType.MESH


def kernel(
    n,
    blocks,
    series_hbm,
    conv_hbm,
    qk_hbm,
    value_hbm,
    out_w_hbm,
    gain_hbm,
    out_ref,
    ext,
    conv_w,
    qk_w,
    kv_w,
    out_w,
    gain,
    gathered,
    key_ref,
    val_ref,
    load_sem,
    halo_send,
    halo_recv,
    peer_send,
    peer_recv,
    fwd_send,
    fwd_recv,
):
    steps, sens, width = out_ref.shape
    taps = conv_w.shape[0]
    lead = taps - 1
    pairs = n // 2
    head_dim = width // HEADS
    factor = math.log2(math.e) / math.sqrt(head_dim)
    me = lax.axis_index("sensor")
    here = lax.axis_index("tm")
    pair, core = me // 2, me % 2
    partner = pair * 2 + 1 - core

    loads = [
        pltpu.make_async_copy(series_hbm, ext.at[pl.ds(lead, steps)], load_sem.at[0]),
        pltpu.make_async_copy(conv_hbm, conv_w, load_sem.at[1]),
        pltpu.make_async_copy(qk_hbm, qk_w, load_sem.at[2]),
        pltpu.make_async_copy(value_hbm, kv_w, load_sem.at[3]),
        pltpu.make_async_copy(out_w_hbm, out_w, load_sem.at[4]),
        pltpu.make_async_copy(gain_hbm, gain, load_sem.at[5]),
    ]
    for load in loads:
        load.start()

    def peer(j):
        return ((pair + j) % pairs) * 2 + core

    barrier = pltpu.get_barrier_semaphore()
    pl.semaphore_signal(barrier, inc=1, device_id={"sensor": partner}, device_id_type=MESH)
    for j in range(1, pairs):
        pl.semaphore_signal(barrier, inc=1, device_id={"sensor": peer(j)}, device_id_type=MESH)

    @pl.when(here > 0)
    def _():
        pl.semaphore_signal(barrier, inc=1, device_id={"tm": here - 1}, device_id_type=MESH)

    @pl.when(here < blocks - 1)
    def _():
        pl.semaphore_signal(barrier, inc=1, device_id={"tm": here + 1}, device_id_type=MESH)

    @pl.when(here == 0)
    def _():
        ext[pl.ds(0, lead)] = jnp.zeros((lead, sens, width), ext.dtype)

    val_ref[:, width:] = jnp.ones((n * sens, width), val_ref.dtype)

    loads[0].wait()
    behind = (here + blocks - 1) // blocks
    ahead = (2 * blocks - 2 - here) // blocks
    pl.semaphore_wait(barrier, pairs + behind + ahead)

    def halo(i):
        return pltpu.make_async_remote_copy(
            src_ref=ext.at[steps + i],
            dst_ref=ext.at[i],
            send_sem=halo_send.at[i],
            recv_sem=halo_recv.at[i],
            device_id={"tm": here + 1},
            device_id_type=MESH,
        )

    @pl.when(here < blocks - 1)
    def _():
        for i in reversed(range(lead)):
            halo(i).start()

    def send(t, j):
        return pltpu.make_async_remote_copy(
            src_ref=gathered.at[t, 0, 0],
            dst_ref=gathered.at[t, 0, j],
            send_sem=peer_send.at[t, j],
            recv_sem=peer_recv.at[t, j],
            device_id={"sensor": peer(j)},
            device_id_type=MESH,
        )

    def forward(t, j):
        return pltpu.make_async_remote_copy(
            src_ref=gathered.at[t, 0, j],
            dst_ref=gathered.at[t, 1, j],
            send_sem=fwd_send.at[t, j],
            recv_sem=fwd_recv.at[t, j],
            device_id={"sensor": partner},
            device_id_type=MESH,
        )

    loads[1].wait()
    for t in reversed(range(steps)):
        if t < lead:

            @pl.when(here > 0)
            def _():
                halo(t).wait_recv()

        conv = jnp.dot(ext[lead + t], conv_w[0], preferred_element_type=jnp.float32)
        for tap in range(1, taps):
            conv = conv + jnp.dot(
                ext[lead + t - tap], conv_w[tap], preferred_element_type=jnp.float32
            )
        own = ext[lead + t].astype(jnp.float32)
        own = own + conv[:, :width] * jax.nn.sigmoid(conv[:, width:])
        gathered[t, 0, 0] = own.astype(gathered.dtype)
        for j in range(1, pairs):
            send(t, j).start()
        forward(t, 0).start()

    for load in loads[2:]:
        load.wait()

    def pass_on(t):
        for j in range(1, pairs):
            send(t, j).wait_recv()
            forward(t, j).start()

    lanes = lax.broadcasted_iota(jnp.int32, (sens, width), 1)
    chunk = min(n * sens, 1024)
    chunks = n * sens // chunk

    def head_parts(query, h):
        mine = (lanes >= h * head_dim) & (lanes < (h + 1) * head_dim)
        masked = jnp.where(mine, query, jnp.zeros_like(query)).astype(jnp.bfloat16)

        def scores_of(c):
            start = c * chunk if isinstance(c, int) else pl.multiple_of(c * chunk, chunk)
            keys = key_ref[pl.ds(start, chunk)]
            scores = lax.dot_general(
                masked, keys, (((1,), (1,)), ((), ())), preferred_element_type=jnp.float32
            )
            return scores, val_ref[pl.ds(start, chunk)]

        if chunks == 1:
            scores, values = scores_of(0)
            top = jnp.max(scores, axis=-1, keepdims=True)
            probs = jnp.exp2((scores - top) * factor).astype(jnp.bfloat16)
            summed = jnp.dot(probs, values, preferred_element_type=jnp.float32)
            return mine, summed

        def one(c, carry):
            maxima, summed = carry
            scores, values = scores_of(c)
            top = jnp.maximum(maxima, jnp.max(scores, axis=-1, keepdims=True))
            probs = jnp.exp2((scores - top) * factor).astype(jnp.bfloat16)
            added = jnp.dot(probs, values, preferred_element_type=jnp.float32)
            return top, summed * jnp.exp2((maxima - top) * factor) + added

        state = (
            jnp.full((sens, 1), -3e38, jnp.float32),
            jnp.zeros((sens, 2 * width), jnp.float32),
        )
        return mine, lax.fori_loop(0, chunks, one, state)[1]

    pass_on(steps - 1)
    for t in reversed(range(steps)):
        for j in range(pairs):
            forward(t, j).wait_recv()
        rows = gathered[t].reshape(n * sens, width)
        key_ref[...] = jnp.dot(rows, qk_w[1], preferred_element_type=jnp.float32).astype(
            jnp.bfloat16
        )
        val_ref[:, :width] = jnp.dot(
            rows, kv_w[...], preferred_element_type=jnp.float32
        ).astype(jnp.bfloat16)
        hidden = gathered[t, 0, 0]
        query = jnp.dot(hidden, qk_w[0], preferred_element_type=jnp.float32)
        query = query.astype(jnp.bfloat16).astype(jnp.float32)
        top_part = jnp.zeros((sens, width), jnp.float32)
        total = jnp.ones((sens, width), jnp.float32)
        for h in range(HEADS):
            if h == HEADS // 2 and t > 0:
                pass_on(t - 1)
            mine, summed = head_parts(query, h)
            top_part = jnp.where(mine, summed[:, :width], top_part)
            total = jnp.where(mine, summed[:, width:], total)
        attended = (top_part / total).astype(jnp.bfloat16)
        mixed = jnp.dot(attended, out_w[...], preferred_element_type=jnp.float32)
        mixed = mixed + hidden.astype(jnp.float32)
        mean = jnp.mean(mixed, axis=-1, keepdims=True)
        centred = mixed - mean
        var = jnp.mean(centred * centred, axis=-1, keepdims=True)
        normed = centred / jnp.sqrt(var + 1e-05) * gain[...]
        out_ref[t] = normed.astype(out_ref.dtype)

    for t in range(steps):
        for j in range(1, pairs):
            send(t, j).wait_send()
        for j in range(pairs):
            forward(t, j).wait_send()

    @pl.when(here < blocks - 1)
    def _():
        for i in range(lead):
            halo(i).wait_send()


def solution(mesh):
    n, blocks = mesh.shape["sensor"], mesh.shape["tm"]

    def local(series, conv_weight, qk_weight, value_weight, out_weight, norm_gain):
        steps, sens, width = series.shape
        taps = conv_weight.shape[0]
        pairs = n // 2
        bf16 = jnp.bfloat16
        return pl.pallas_call(
            functools.partial(kernel, n, blocks),
            out_shape=jax.ShapeDtypeStruct(series.shape, bf16),
            in_specs=[pl.BlockSpec(memory_space=pl.ANY)] * 6,
            out_specs=pl.BlockSpec(memory_space=pltpu.VMEM),
            scratch_shapes=[
                pltpu.VMEM((taps - 1 + steps, sens, width), bf16),
                pltpu.VMEM(conv_weight.shape, bf16),
                pltpu.VMEM(qk_weight.shape, bf16),
                pltpu.VMEM(value_weight.shape, bf16),
                pltpu.VMEM(out_weight.shape, bf16),
                pltpu.VMEM((1, width), jnp.float32),
                pltpu.VMEM((steps, 2, pairs, sens, width), bf16),
                pltpu.VMEM((n * sens, width), bf16),
                pltpu.VMEM((n * sens, 2 * width), bf16),
                pltpu.SemaphoreType.DMA((6,)),
                pltpu.SemaphoreType.DMA((taps - 1,)),
                pltpu.SemaphoreType.DMA((taps - 1,)),
                pltpu.SemaphoreType.DMA((steps, pairs)),
                pltpu.SemaphoreType.DMA((steps, pairs)),
                pltpu.SemaphoreType.DMA((steps, pairs)),
                pltpu.SemaphoreType.DMA((steps, pairs)),
            ],
            compiler_params=pltpu.CompilerParams(collective_id=0, has_side_effects=True),
        )(
            series,
            conv_weight,
            qk_weight,
            value_weight,
            out_weight,
            norm_gain.reshape(1, width),
        )

    in_specs = (P("tm", "sensor", None), P(), P(), P(), P(), P())
    out_specs = P("tm", "sensor", None)
    return jax.shard_map(local, mesh=mesh, in_specs=in_specs, out_specs=out_specs, check_vma=False)
```

time: 45 us -> 19.3 us (0.43)
  blocking collectives: 20.8 us -> 0 us
  Pallas kernels: 0 us -> 17.5 us
  matrix products: 10.5 us -> 0 us
  starting transfers between devices: 4.95 us -> 0 us
  other arithmetic: 4.22 us -> 0 us
  local copies, waits for them, and re-layouts: 2.89 us -> 1.54 us
  waiting for transfers between devices: 0.77 us -> 0 us
    all_gather x2 -> x0, blocking collectives: 20.8 us -> none  [the longest x1 10.4 us: local(): keys = lax.all_gather(own_keys, 'sensor', axis=1, tiled=True)]
    pallas_call x0 -> x1, Pallas kernels: none -> 17.5 us  [local(): pl.pallas_call(functools.partial(kernel, n, blocks), out_shape=jax.ShapeD...]
    dot_general x11 -> x0, matrix products: 10.5 us -> none  [the longest x3 3.13 us: local(): jnp.dot(window, conv_weight[tap], preferred_element_type=jnp.float32)]
    ppermute x1 -> x0, starting transfers between devices: 4.95 us -> none  [from_behind(): return lax.ppermute(block, axis, route)]
    reduce_sum x3 -> x0, other arithmetic: 2.35 us -> none  [the longest x2 2.12 us: absorb_block(): totals = totals * correct + jnp.sum(probs, axis=-1)]
    convert_element_type x3 -> x0, other arithmetic: 1.8 us -> none  [the longest x1 0.96 us: local(): (flat + conv[:, :width] * jax.nn.sigmoid(conv[:, width:])).astype(jnp.bfl...]
    unnamed x6 -> x1, local copies, waits for them, and re-layouts: 0.03 us -> 1.54 us
    concatenate x1 -> x0, local copies, waits for them, and re-layouts: 0.91 us -> none  [local(): padded = jnp.concatenate([earlier, series], axis=0)]
  transfers between devices with their start and end apart: 1 -> 0, of which waited for: 1 -> 0; matrix products, arithmetic and copies ran while one was open for 2% -> 0% of each run, Pallas kernels for 0% -> 0%
where the time goes in v1:
time: 19.3 us; the launch traced here: 19.1 us
  Pallas kernels  17.5 us (91%)
  local copies, waits for them, and re-layouts  1.54 us (8%)
    pallas_call x1, Pallas kernels, local(): pl.pallas_call(functools.partial(kernel, n, blocks), out_shape=jax.ShapeD...  17.5 us
    unnamed x1, local copies, waits for them, and re-layouts  1.54 us

profile of v1, /device:TPU:0, one launch (start us, length us, event | category | flops | bytes accessed | tf_op | source)
XLA Modules:
  0.0 19.1 jit_solution(15240051579728604619)
XLA Ops:
  0.0 17.5 %shard_map.64 = bf16[3,128,128]{2,1,0:T(8,128)(2,1)} custom-call(bf16[3,128,128]{2,1,0:T(8,128)(2,1)} %series_hbm.1, bf16[3,128,256]{2,1,0:T(8,128)(2,1)} %conv_hbm.1, bf16[2,128,128]{2,1,0:T(8,128)(2,1)} %qk_hbm.1, bf16[128,128]{1,0:T(8,128)(2,1)} %value_hbm.1, bf16[128,128]{1,0:T(8,128)(2,1)} %out_w_hbm.1, f32[1,128]{1,0:T(1,128)} %bitcast.1), custom_call_target="tpu_custom_call" | custom-call | tf_op jit(solution)/shard_map/pallas_call | solution.py:242
  17.5 1.5 %copy.8 = bf16[3,128,128]{2,1,0:T(8,128)(2,1)} copy(bf16[3,128,128]{2,1,0:T(8,128)(2,1)} %shard_map.64) | data formatting | bytes 196608

commit v2 on v1

--- a/solution.py
+++ b/solution.py
@@ -24,11 +24,12 @@
     out_ref,
     ext,
     conv_w,
-    qk_w,
+    q_w,
     kv_w,
     out_w,
     gain,
     gathered,
+    query_ref,
     key_ref,
     val_ref,
     load_sem,
@@ -53,10 +54,11 @@
     loads = [
         pltpu.make_async_copy(series_hbm, ext.at[pl.ds(lead, steps)], load_sem.at[0]),
         pltpu.make_async_copy(conv_hbm, conv_w, load_sem.at[1]),
-        pltpu.make_async_copy(qk_hbm, qk_w, load_sem.at[2]),
-        pltpu.make_async_copy(value_hbm, kv_w, load_sem.at[3]),
-        pltpu.make_async_copy(out_w_hbm, out_w, load_sem.at[4]),
-        pltpu.make_async_copy(gain_hbm, gain, load_sem.at[5]),
+        pltpu.make_async_copy(qk_hbm.at[0], q_w, load_sem.at[2]),
+        pltpu.make_async_copy(qk_hbm.at[1], kv_w.at[:, pl.ds(0, width)], load_sem.at[3]),
+        pltpu.make_async_copy(value_hbm, kv_w.at[:, pl.ds(width, width)], load_sem.at[4]),
+        pltpu.make_async_copy(out_w_hbm, out_w, load_sem.at[5]),
+        pltpu.make_async_copy(gain_hbm, gain, load_sem.at[6]),
     ]
     for load in loads:
         load.start()
@@ -81,7 +83,7 @@
     def _():
         ext[pl.ds(0, lead)] = jnp.zeros((lead, sens, width), ext.dtype)
 
-    val_ref[:, width:] = jnp.ones((n * sens, width), val_ref.dtype)
+    val_ref[:, :, width:] = jnp.ones((steps, n * sens, width), val_ref.dtype)
 
     loads[0].wait()
     behind = (here + blocks - 1) // blocks
@@ -106,7 +108,7 @@
     def send(t, j):
         return pltpu.make_async_remote_copy(
             src_ref=gathered.at[t, 0, 0],
-            dst_ref=gathered.at[t, 0, j],
+            dst_ref=gathered.at[t, j, 0],
             send_sem=peer_send.at[t, j],
             recv_sem=peer_recv.at[t, j],
             device_id={"sensor": peer(j)},
@@ -115,16 +117,18 @@
 
     def forward(t, j):
         return pltpu.make_async_remote_copy(
-            src_ref=gathered.at[t, 0, j],
-            dst_ref=gathered.at[t, 1, j],
+            src_ref=gathered.at[t, j, 0],
+            dst_ref=gathered.at[t, j, 1],
             send_sem=fwd_send.at[t, j],
             recv_sem=fwd_recv.at[t, j],
             device_id={"sensor": partner},
             device_id_type=MESH,
         )
 
-    loads[1].wait()
-    for t in reversed(range(steps)):
+    lanes = lax.broadcasted_iota(jnp.int32, (sens, width), 1)
+    mine = [(lanes >= h * head_dim) & (lanes < (h + 1) * head_dim) for h in range(HEADS)]
+
+    def prepare(t):
         if t < lead:
 
             @pl.when(here > 0)
@@ -143,81 +147,100 @@
             send(t, j).start()
         forward(t, 0).start()
 
-    for load in loads[2:]:
-        load.wait()
+    def queries(t):
+        query = jnp.dot(gathered[t, 0, 0], q_w[...], preferred_element_type=jnp.float32)
+        for h in range(HEADS):
+            query_ref[t, h] = jnp.where(mine[h], query, 0.0).astype(jnp.bfloat16)
 
     def pass_on(t):
         for j in range(1, pairs):
             send(t, j).wait_recv()
             forward(t, j).start()
 
-    lanes = lax.broadcasted_iota(jnp.int32, (sens, width), 1)
-    chunk = min(n * sens, 1024)
-    chunks = n * sens // chunk
-
-    def head_parts(query, h):
-        mine = (lanes >= h * head_dim) & (lanes < (h + 1) * head_dim)
-        masked = jnp.where(mine, query, jnp.zeros_like(query)).astype(jnp.bfloat16)
-
-        def scores_of(c):
-            start = c * chunk if isinstance(c, int) else pl.multiple_of(c * chunk, chunk)
-            keys = key_ref[pl.ds(start, chunk)]
+    def absorb(t, rows, start):
+        count = rows.shape[0]
+        place = pl.ds(start, count)
+        both = jnp.dot(rows, kv_w[...], preferred_element_type=jnp.float32)
+        key_ref[t, place] = both[:, :width].astype(jnp.bfloat16)
+        val_ref[t, place, :width] = both[:, width:].astype(jnp.bfloat16)
+        maxima = weighted = total = jnp.zeros((sens, width), jnp.float32)
+        for h in range(HEADS):
             scores = lax.dot_general(
-                masked, keys, (((1,), (1,)), ((), ())), preferred_element_type=jnp.float32
+                query_ref[t, h],
+                key_ref[t, place],
+                (((1,), (1,)), ((), ())),
+                preferred_element_type=jnp.float32,
             )
-            return scores, val_ref[pl.ds(start, chunk)]
-
-        if chunks == 1:
-            scores, values = scores_of(0)
             top = jnp.max(scores, axis=-1, keepdims=True)
             probs = jnp.exp2((scores - top) * factor).astype(jnp.bfloat16)
-            summed = jnp.dot(probs, values, preferred_element_type=jnp.float32)
-            return mine, summed
-
-        def one(c, carry):
-            maxima, summed = carry
-            scores, values = scores_of(c)
-            top = jnp.maximum(maxima, jnp.max(scores, axis=-1, keepdims=True))
-            probs = jnp.exp2((scores - top) * factor).astype(jnp.bfloat16)
-            added = jnp.dot(probs, values, preferred_element_type=jnp.float32)
-            return top, summed * jnp.exp2((maxima - top) * factor) + added
-
-        state = (
-            jnp.full((sens, 1), -3e38, jnp.float32),
-            jnp.zeros((sens, 2 * width), jnp.float32),
-        )
-        return mine, lax.fori_loop(0, chunks, one, state)[1]
-
-    pass_on(steps - 1)
-    for t in reversed(range(steps)):
-        for j in range(pairs):
-            forward(t, j).wait_recv()
-        rows = gathered[t].reshape(n * sens, width)
-        key_ref[...] = jnp.dot(rows, qk_w[1], preferred_element_type=jnp.float32).astype(
-            jnp.bfloat16
-        )
-        val_ref[:, :width] = jnp.dot(
-            rows, kv_w[...], preferred_element_type=jnp.float32
-        ).astype(jnp.bfloat16)
-        hidden = gathered[t, 0, 0]
-        query = jnp.dot(hidden, qk_w[0], preferred_element_type=jnp.float32)
-        query = query.astype(jnp.bfloat16).astype(jnp.float32)
-        top_part = jnp.zeros((sens, width), jnp.float32)
-        total = jnp.ones((sens, width), jnp.float32)
-        for h in range(HEADS):
-            if h == HEADS // 2 and t > 0:
-                pass_on(t - 1)
-            mine, summed = head_parts(query, h)
-            top_part = jnp.where(mine, summed[:, :width], top_part)
-            total = jnp.where(mine, summed[:, width:], total)
-        attended = (top_part / total).astype(jnp.bfloat16)
+            summed = jnp.dot(probs, val_ref[t, place], preferred_element_type=jnp.float32)
+            maxima = jnp.where(mine[h], top, maxima)
+            weighted = jnp.where(mine[h], summed[:, :width], weighted)
+            total = jnp.where(mine[h], summed[:, width:], total)
+        return maxima, weighted, total
+
+    def merge(states):
+        maxima = functools.reduce(jnp.maximum, [state[0] for state in states])
+        weighted = total = 0.0
+        for state in states:
+            share = jnp.exp2((state[0] - maxima) * factor)
+            weighted = weighted + state[1] * share
+            total = total + state[2] * share
+        return maxima, weighted, total
+
+    states = [[] for _ in range(steps)]
+
+    def near(t):
+        forward(t, 0).wait_recv()
+        states[t].append(absorb(t, gathered[t, 0].reshape(2 * sens, width), 0))
+
+    def far(t, side):
+        if side:
+            for j in range(1, pairs):
+                forward(t, j).wait_recv()
+        if pairs <= 4:
+            rows = gathered[t, pl.ds(1, pairs - 1), side].reshape((pairs - 1) * sens, width)
+            start = (2 + side * (pairs - 1)) * sens
+            states[t].append(absorb(t, rows, start))
+            return
+
+        def one(j, state):
+            return merge([state, absorb(t, gathered[t, j, side], 0)])
+
+        states[t] = [lax.fori_loop(1, pairs, one, merge(states[t]))]
+
+    def finish(t):
+        _, weighted, total = merge(states[t])
+        attended = (weighted / total).astype(jnp.bfloat16)
         mixed = jnp.dot(attended, out_w[...], preferred_element_type=jnp.float32)
-        mixed = mixed + hidden.astype(jnp.float32)
+        mixed = mixed + gathered[t, 0, 0].astype(jnp.float32)
         mean = jnp.mean(mixed, axis=-1, keepdims=True)
         centred = mixed - mean
         var = jnp.mean(centred * centred, axis=-1, keepdims=True)
         normed = centred / jnp.sqrt(var + 1e-05) * gain[...]
         out_ref[t] = normed.astype(out_ref.dtype)
+
+    last = steps - 1
+    loads[1].wait()
+    prepare(last)
+    for load in loads[2:]:
+        load.wait()
+    queries(last)
+    near(last)
+    for t in reversed(range(last)):
+        prepare(t)
+        queries(t)
+    if last > 0:
+        near(last - 1)
+    pass_on(last)
+    for t in reversed(range(last - 1)):
+        near(t)
+    for t in reversed(range(steps)):
+        far(t, 0)
+        far(t, 1)
+        if t > 0:
+            pass_on(t - 1)
+        finish(t)
 
     for t in range(steps):
         for j in range(1, pairs):
@@ -247,14 +270,15 @@
             scratch_shapes=[
                 pltpu.VMEM((taps - 1 + steps, sens, width), bf16),
                 pltpu.VMEM(conv_weight.shape, bf16),
-                pltpu.VMEM(qk_weight.shape, bf16),
-                pltpu.VMEM(value_weight.shape, bf16),
+                pltpu.VMEM((width, width), bf16),
+                pltpu.VMEM((width, 2 * width), bf16),
                 pltpu.VMEM(out_weight.shape, bf16),
                 pltpu.VMEM((1, width), jnp.float32),
-                pltpu.VMEM((steps, 2, pairs, sens, width), bf16),
-                pltpu.VMEM((n * sens, width), bf16),
-                pltpu.VMEM((n * sens, 2 * width), bf16),
-                pltpu.SemaphoreType.DMA((6,)),
+                pltpu.VMEM((steps, pairs, 2, sens, width), bf16),
+                pltpu.VMEM((steps, HEADS, sens, width), bf16),
+                pltpu.VMEM((steps, n * sens, width), bf16),
+                pltpu.VMEM((steps, n * sens, 2 * width), bf16),
+                pltpu.SemaphoreType.DMA((7,)),
                 pltpu.SemaphoreType.DMA((taps - 1,)),
                 pltpu.SemaphoreType.DMA((taps - 1,)),
                 pltpu.SemaphoreType.DMA((steps, pairs)),

time: 19.3 us -> 19 us (0.984)
  Pallas kernels: 17.5 us -> 17.3 us
    pallas_call x1, Pallas kernels: 17.5 us -> 17.3 us  [local(): pl.pallas_call(functools.partial(kernel, n, blocks), out_shape=jax.ShapeD...]
where the time goes in v2:
time: 19 us; the launch traced here: 18.8 us
  Pallas kernels  17.3 us (91%)
  local copies, waits for them, and re-layouts  1.54 us (8%)
    pallas_call x1, Pallas kernels, local(): pl.pallas_call(functools.partial(kernel, n, blocks), out_shape=jax.ShapeD...  17.3 us
    unnamed x1, local copies, waits for them, and re-layouts  1.54 us

profile of v2, /device:TPU:0, one launch (start us, length us, event | category | flops | bytes accessed | tf_op | source)
XLA Modules:
  0.0 18.8 jit_solution(1916829156867748328)
XLA Ops:
  0.0 17.3 %shard_map.64 = bf16[3,128,128]{2,1,0:T(8,128)(2,1)} custom-call(bf16[3,128,128]{2,1,0:T(8,128)(2,1)} %series_hbm.1, bf16[3,128,256]{2,1,0:T(8,128)(2,1)} %conv_hbm.1, bf16[2,128,128]{2,1,0:T(8,128)(2,1)} %qk_hbm.1, bf16[128,128]{1,0:T(8,128)(2,1)} %value_hbm.1, bf16[128,128]{1,0:T(8,128)(2,1)} %out_w_hbm.1, f32[1,128]{1,0:T(1,128)} %bitcast.1), custom_call_target="tpu_custom_call" | custom-call | tf_op jit(solution)/shard_map/pallas_call | solution.py:265
  17.3 1.5 %copy.8 = bf16[3,128,128]{2,1,0:T(8,128)(2,1)} copy(bf16[3,128,128]{2,1,0:T(8,128)(2,1)} %shard_map.64) | data formatting | bytes 196608

commit v3 on v2

--- a/solution.py
+++ b/solution.py
@@ -190,24 +190,20 @@
 
     states = [[] for _ in range(steps)]
 
-    def near(t):
-        forward(t, 0).wait_recv()
-        states[t].append(absorb(t, gathered[t, 0].reshape(2 * sens, width), 0))
-
-    def far(t, side):
+    def half(t, side):
         if side:
-            for j in range(1, pairs):
+            for j in range(pairs):
                 forward(t, j).wait_recv()
         if pairs <= 4:
-            rows = gathered[t, pl.ds(1, pairs - 1), side].reshape((pairs - 1) * sens, width)
-            start = (2 + side * (pairs - 1)) * sens
-            states[t].append(absorb(t, rows, start))
+            rows = gathered[t, :, side].reshape(pairs * sens, width)
+            states[t].append(absorb(t, rows, side * pairs * sens))
             return
 
         def one(j, state):
             return merge([state, absorb(t, gathered[t, j, side], 0)])
 
-        states[t] = [lax.fori_loop(1, pairs, one, merge(states[t]))]
+        start = absorb(t, gathered[t, 0, side], 0)
+        states[t].append(lax.fori_loop(1, pairs, one, start))
 
     def finish(t):
         _, weighted, total = merge(states[t])
@@ -226,18 +222,13 @@
     for load in loads[2:]:
         load.wait()
     queries(last)
-    near(last)
     for t in reversed(range(last)):
         prepare(t)
         queries(t)
-    if last > 0:
-        near(last - 1)
     pass_on(last)
-    for t in reversed(range(last - 1)):
-        near(t)
     for t in reversed(range(steps)):
-        far(t, 0)
-        far(t, 1)
+        half(t, 0)
+        half(t, 1)
         if t > 0:
             pass_on(t - 1)
         finish(t)

time: 19 us -> 19 us (level)
  no operation moved by 1% of the time
where the time goes in v3:
time: 19 us; the launch traced here: 18.8 us
  Pallas kernels  17.3 us (91%)
  local copies, waits for them, and re-layouts  1.54 us (8%)
    pallas_call x1, Pallas kernels, local(): pl.pallas_call(functools.partial(kernel, n, blocks), out_shape=jax.ShapeD...  17.3 us
    unnamed x1, local copies, waits for them, and re-layouts  1.54 us

profile of v3, /device:TPU:0, one launch (start us, length us, event | category | flops | bytes accessed | tf_op | source)
XLA Modules:
  0.0 18.8 jit_solution(8304692242445477152)
XLA Ops:
  0.0 17.3 %shard_map.64 = bf16[3,128,128]{2,1,0:T(8,128)(2,1)} custom-call(bf16[3,128,128]{2,1,0:T(8,128)(2,1)} %series_hbm.1, bf16[3,128,256]{2,1,0:T(8,128)(2,1)} %conv_hbm.1, bf16[2,128,128]{2,1,0:T(8,128)(2,1)} %qk_hbm.1, bf16[128,128]{1,0:T(8,128)(2,1)} %value_hbm.1, bf16[128,128]{1,0:T(8,128)(2,1)} %out_w_hbm.1, f32[1,128]{1,0:T(1,128)} %bitcast.1), custom_call_target="tpu_custom_call" | custom-call | tf_op jit(solution)/shard_map/pallas_call | solution.py:256
  17.3 1.5 %copy.8 = bf16[3,128,128]{2,1,0:T(8,128)(2,1)} copy(bf16[3,128,128]{2,1,0:T(8,128)(2,1)} %shard_map.64) | data formatting | bytes 196608
